TPU v7x, 32 devices: a whole 2x2x4 slice. The times are simulated.
32 devices in a mesh: groups: 2 (over y), tm: 4 (over z), chan: 2 (over x), sub: 2 (over core).
Axes of the slice: x: 2, y: 2, z: 4, core: 2. Of those that a mesh axis runs over, the one named last changes fastest.
Arguments:
- signal: bfloat16 [2, 240, 65536], P(None, 'chan', ('groups', 'tm', 'sub')), parts along dimension 2, may hold values from -6 to 6
- channel_mask: int32 [240], P('chan'), may hold values from 0 to 1, as said below
- dispersion: float32 [240], P('chan'), may hold values from 1228.8 to 12288
- equaliser: bfloat16 [96, 2, 240, 240], P(('tm', 'chan')), may hold values from -0.25 to 0.25
- bin_block: int32 [64, 128], P(None, ('tm', 'chan')), may hold values from 0 to 11
Outputs:
- output: bfloat16 [2, 240, 65536], P(None, 'chan', ('groups', 'tm', 'sub')), parts along dimension 2
There are 2 independent parts, one for each index of `groups`. A program takes and returns all parts, laid end to end along the dimension named above; an argument that names none is the same for every part. Nothing has to cross between parts.
Inputs may be any that keep to these rules, and one draw needn't show every extreme that they name: `channel_mask`: exactly 228 entries are 1.
All inputs are finite; a program needn't handle non-finite values.
Results may differ from a plain program's by a relative error of at most 0.0089.
Values may be sent and summed in bfloat16 or wider, within the bound.
No kernel may reach another device: no remote copies, remote signals or barrier semaphores. Data moves between devices by JAX's collectives and lax.ppermute only.
A program may use at most 128 MiB of HBM per device.

v0:
```python
import math

import jax
import jax.numpy as jnp
from jax import lax
from jax.sharding import PartitionSpec as P

TAPS = 4096
N1 = 128
NFFT = 8192
N2 = 64


def from_behind(value, axis, by):
    devices = lax.axis_size(axis)
    pairs = [(i, i + by) for i in range(devices) if 0 <= i + by < devices]
    return lax.ppermute(value, axis, pairs)


def dft_table(length, inverse):
    counter = jnp.arange(length, dtype=jnp.int32)
    product = counter[:, None] * counter[None, :] % length
    angle = product.astype(jnp.float32) * (2.0 * math.pi / length)
    factor = 1.0 / math.sqrt(length)
    cosine = jnp.cos(angle) * factor
    sine = jnp.sin(angle) * factor
    if inverse:
        upper = jnp.stack([cosine, -sine], axis=1)
        lower = jnp.stack([sine, cosine], axis=1)
    else:
        upper = jnp.stack([cosine, sine], axis=1)
        lower = jnp.stack([-sine, cosine], axis=1)
    return jnp.stack([upper, lower], axis=0).astype(jnp.bfloat16)


def twist_table(first_rows, columns):
    seconds = jnp.arange(columns, dtype=jnp.int32)
    product = first_rows[:, None] * seconds[None, :] % NFFT
    angle = product.astype(jnp.float32) * (2.0 * math.pi / NFFT)
    return (jnp.cos(angle), jnp.sin(angle))


def phase_table(dispersion):
    first_rows = jnp.arange(N1, dtype=jnp.int32)
    seconds = jnp.arange(N2, dtype=jnp.int32)
    bins = first_rows[:, None] + N1 * seconds[None, :]
    centred = jnp.where(bins < NFFT // 2, bins, bins - NFFT)
    freq_sq = (centred * centred).astype(jnp.float32) / float(NFFT * NFFT)
    quarter = jnp.mod(centred, 4).astype(jnp.float32) * (0.5 * math.pi)
    phase = dispersion[:, None, None] * freq_sq[None] - quarter[None]
    return (jnp.cos(phase), jnp.sin(phase))


def invert_second(spectra, first_rows, inverse_second):
    partial_value = jnp.einsum(
        "rspk,cjfpk->cjfrs", inverse_second, spectra, preferred_element_type=jnp.float32
    )
    cos_inv, sin_inv = twist_table(first_rows, N2)
    cos_inv = cos_inv[:, None, :]
    sin_inv = sin_inv[:, None, :]
    real_g = partial_value[:, :, :, 0]
    imag_g = partial_value[:, :, :, 1]
    turned = jnp.stack(
        [real_g * cos_inv - imag_g * sin_inv, imag_g * cos_inv + real_g * sin_inv], axis=3
    )
    return turned.astype(jnp.bfloat16)


def on_device(signal, channel_mask, dispersion, equaliser, bin_block):
    channels_dev = signal.shape[1]
    frame_count = signal.shape[2] // TAPS
    half_rows = N1 // 2
    mask_half = channel_mask.astype(jnp.bfloat16)
    masked = signal * mask_half[None, :, None]
    tail_in = from_behind(masked, ("tm", "sub"), 1)
    forward_first = dft_table(N1, False)
    forward_second = dft_table(N2, False)
    inverse_first = dft_table(N1, True)
    inverse_second = dft_table(N2, True)
    own_halves = masked.reshape(2, channels_dev, frame_count, TAPS)
    previous = jnp.concatenate([tail_in[:, :, None], own_halves[:, :, :-1]], axis=2)
    frames = jnp.concatenate([previous, own_halves], axis=3).reshape(
        2, channels_dev, frame_count, N1, N2
    )
    section_a = jnp.einsum(
        "pkqt,qcfts->cfpks", forward_first, frames, preferred_element_type=jnp.float32
    )
    cos_twist, sin_twist = twist_table(jnp.arange(N1, dtype=jnp.int32), N2)
    real_a = section_a[:, :, 0]
    imag_a = section_a[:, :, 1]
    twisted = jnp.stack(
        [real_a * cos_twist + imag_a * sin_twist, imag_a * cos_twist - real_a * sin_twist], axis=2
    ).astype(jnp.bfloat16)
    spectrum = jnp.einsum(
        "rlps,cfpks->ckfrl", forward_second, twisted, preferred_element_type=jnp.float32
    )
    cos_disp, sin_disp = phase_table(dispersion)
    cos_disp = cos_disp[:, :, None, :]
    sin_disp = sin_disp[:, :, None, :]
    real_s = spectrum[:, :, :, 0]
    imag_s = spectrum[:, :, :, 1]
    dispersed = jnp.stack(
        [real_s * cos_disp - imag_s * sin_disp, real_s * sin_disp + imag_s * cos_disp], axis=3
    )
    dispersed = dispersed.astype(jnp.bfloat16).reshape(channels_dev, N1, frame_count, 2 * N2)
    by_bins = lax.all_to_all(dispersed, ("tm", "chan"), split_axis=1, concat_axis=1, tiled=True)
    tm_count = lax.axis_size("tm")
    chan_count = lax.axis_size("chan")
    bins_rows = N1 // (tm_count * chan_count)
    grid = by_bins.reshape(channels_dev, tm_count, chan_count, bins_rows, frame_count, 2, N2)
    shaped_weights = equaliser.reshape(
        equaliser.shape[0], 2, chan_count, channels_dev, chan_count, channels_dev
    )
    group_size = 8

    def equalise_group(group_step, result):
        start = group_step * group_size
        columns = lax.dynamic_slice_in_dim(grid, start, group_size, 6)
        picks = lax.dynamic_slice_in_dim(bin_block, start, group_size, 0)
        chosen = jnp.take(shaped_weights, picks, axis=0)
        mixed = jnp.einsum(
            "gjsxyad,dtajfqg->ytxjfsqg", chosen, columns, preferred_element_type=jnp.float32
        )
        real_e = mixed[:, :, :, :, :, 0, 0] - mixed[:, :, :, :, :, 1, 1]
        imag_e = mixed[:, :, :, :, :, 0, 1] + mixed[:, :, :, :, :, 1, 0]
        block_out = jnp.stack([real_e, imag_e], axis=5).astype(jnp.bfloat16)
        return lax.dynamic_update_slice_in_dim(result, block_out, start, 6)

    equalised = lax.fori_loop(
        0, N2 // group_size, equalise_group, jnp.zeros(grid.shape, jnp.bfloat16)
    )
    equalised = equalised.reshape(channels_dev, N1, frame_count, 2, N2)
    returned = lax.all_to_all(
        equalised.reshape(channels_dev, N1, frame_count, 2 * N2),
        ("tm", "chan"),
        split_axis=1,
        concat_axis=1,
        tiled=True,
    )
    returned = returned.reshape(channels_dev, N1, frame_count, 2, N2)
    restored = invert_second(returned, jnp.arange(N1, dtype=jnp.int32), inverse_second)
    values = jnp.einsum(
        "rupj,cjfpt->rcfut",
        inverse_first[:, half_rows:],
        restored,
        preferred_element_type=jnp.float32,
    )
    values = values.reshape(2, channels_dev, frame_count * TAPS)
    return (values * channel_mask.astype(jnp.float32)[None, :, None]).astype(jnp.bfloat16)


def solution(mesh):
    in_specs = (
        P(None, "chan", ("groups", "tm", "sub")),
        P("chan"),
        P("chan"),
        P(("tm", "chan"), None, None, None),
        P(None, ("tm", "chan")),
    )
    out_specs = P(None, "chan", ("groups", "tm", "sub"))
    return jax.shard_map(
        on_device, mesh=mesh, in_specs=in_specs, out_specs=out_specs, check_vma=False
    )
```

profile of v0, /device:TPU:20, one launch (start us, length us, event | category | flops | bytes accessed | tf_op | source)
XLA Modules:
  0.0 994.0 jit_solution(6519776769160690254)
XLA Ops:
  9.4 7.1 copy.80
  19.0 11.6 %collective-permute-done = bf16[2,120,4096]{2,1,0:T(8,128)(2,1)} collective-permute-done((bf16[2,120,4096]{2,1,0:T(8,128)(2,1)}, bf16[2,120,4096]{2,1,0:T(8,128)(2,1)}, u32[]{:S(2)}, u32[]{:S(2)}) %collective-permute-start) | collective-permute-done | bytes 1966112 | tf_op jit(solution)/shard_map/ppermute | solution.py:17
  33.7 7.2 copy.79
  49.7 15.6 %subtract_convert_fusion = (bf16[120,128,1,1,64]{1,4,3,0,2:T(8,128)(2,1)S(1)}, bf16[120,128,1,1,64]{1,4,3,0,2:T(8,128)(2,1)S(1)}) fusion(f32[120,128,1,2,64]{1,4,3,0,2:T(8,128)S(1)} %fusion.28, f32[128,64]{0,1:T(8,128)S(1)} %get-tuple-element.149, f32[128,64]{0,1:T(8,128)S(1)} %get-tuple-element.148, f32[120]{0:T(128)S(1)} %copy-done.9), kind=kLoop, calls=%fused_computation.50 | loop fusion | flops 9830400 | bytes 11862496 | tf_op jit(solution)/shard_map/convert.24
  86.8 76.2 %all-to-all-done = bf16[120,128,1,128]{3,0,2,1:T(8,128)(2,1)} async-done(((bf16[120,128,1,128]{3,0,2,1:T(8,128)(2,1)}), bf16[120,128,1,128]{3,0,2,1:T(8,128)(2,1)}, u32[]{:S(2)}, u32[]{:S(2)}) %all-to-all-start) | async-done | bytes 3932192 | tf_op jit(solution)/shard_map/all_to_all | solution.py:106
  172.4 692.1 %while.13 = (s32[]{:T(128)}, bf16[120,4,2,16,1,2,64]{0,6,5,3,2,1,4:T(8,128)(2,1)}, bf16[120,4,2,16,1,2,64]{0,6,5,3,2,1,4:T(8,128)(2,1)}, s32[64,16]{1,0:T(8,128)...) while((s32[]{:T(128)}, ...), condition=%wide.region_1.2_spmd, body=%wide.region_0.1_spmd.sunk | while | flops 251414272 | bytes 96378512 | solution.py:129
  173.6 64.6 %gather_fusion = bf16[128,2,2,120,2,120]{5,4,3,2,1,0:T(2,128)(2,1)} fusion(bf16[12,2,2,120,2,120]{5,4,3,2,1,0:T(2,128)(2,1)S(1)} %get-tuple-element.213, s32[1024]{0:T(1024)S(1)} %pad_clamp_fusion.2), kind=kCustom, calls=%fused_computation.clone.1 | custom fusion | bytes 58982912 | tf_op jit(solution)/shard_map/while/body/eval_jaxpr/jit(_take)/gather | solution.py:120
  238.2 19.0 %fusion.92 = f32[120,4,2,16,1,2,2,8]{0,1,2,5,6,7,3,4:T(4,128)S(1)} fusion(bf16[8,16,2,2,120,2,120]{6,5,4,3,2,1,0:T(2,128)(2,1)} %bitcast.201, pred[8,16]{0,1:T(8,128)(4,1)S(1)} %copy.146, bf16[120,4,2,16,1,2,8]{0,6,5,3,2,1,4:T(8,128)(2,1)S(1)} %constant_dynamic-slice_fusion.2), kind=kOutput, calls=%fused_computation.6.clone.1 | convolution fusion | flops 250675200 | bytes 31948928 | tf_op jit(solution)/shard_map/while/body/eval_jaxpr/gjsxyad,dtajfqg->ytxjfsqg/dot_general | solution.py:121
  260.2 64.6 %gather_fusion = bf16[128,2,2,120,2,120]{5,4,3,2,1,0:T(2,128)(2,1)} fusion(bf16[12,2,2,120,2,120]{5,4,3,2,1,0:T(2,128)(2,1)S(1)} %get-tuple-element.213, s32[1024]{0:T(1024)S(1)} %pad_clamp_fusion.2), kind=kCustom, calls=%fused_computation.clone.1 | custom fusion | bytes 58982912 | tf_op jit(solution)/shard_map/while/body/eval_jaxpr/jit(_take)/gather | solution.py:120
  324.8 19.0 %fusion.92 = f32[120,4,2,16,1,2,2,8]{0,1,2,5,6,7,3,4:T(4,128)S(1)} fusion(bf16[8,16,2,2,120,2,120]{6,5,4,3,2,1,0:T(2,128)(2,1)} %bitcast.201, pred[8,16]{0,1:T(8,128)(4,1)S(1)} %copy.146, bf16[120,4,2,16,1,2,8]{0,6,5,3,2,1,4:T(8,128)(2,1)S(1)} %constant_dynamic-slice_fusion.2), kind=kOutput, calls=%fused_computation.6.clone.1 | convolution fusion | flops 250675200 | bytes 31948928 | tf_op jit(solution)/shard_map/while/body/eval_jaxpr/gjsxyad,dtajfqg->ytxjfsqg/dot_general | solution.py:121
  346.7 64.6 %gather_fusion = bf16[128,2,2,120,2,120]{5,4,3,2,1,0:T(2,128)(2,1)} fusion(bf16[12,2,2,120,2,120]{5,4,3,2,1,0:T(2,128)(2,1)S(1)} %get-tuple-element.213, s32[1024]{0:T(1024)S(1)} %pad_clamp_fusion.2), kind=kCustom, calls=%fused_computation.clone.1 | custom fusion | bytes 58982912 | tf_op jit(solution)/shard_map/while/body/eval_jaxpr/jit(_take)/gather | solution.py:120
  411.3 19.0 %fusion.92 = f32[120,4,2,16,1,2,2,8]{0,1,2,5,6,7,3,4:T(4,128)S(1)} fusion(bf16[8,16,2,2,120,2,120]{6,5,4,3,2,1,0:T(2,128)(2,1)} %bitcast.201, pred[8,16]{0,1:T(8,128)(4,1)S(1)} %copy.146, bf16[120,4,2,16,1,2,8]{0,6,5,3,2,1,4:T(8,128)(2,1)S(1)} %constant_dynamic-slice_fusion.2), kind=kOutput, calls=%fused_computation.6.clone.1 | convolution fusion | flops 250675200 | bytes 31948928 | tf_op jit(solution)/shard_map/while/body/eval_jaxpr/gjsxyad,dtajfqg->ytxjfsqg/dot_general | solution.py:121
  433.2 64.6 %gather_fusion = bf16[128,2,2,120,2,120]{5,4,3,2,1,0:T(2,128)(2,1)} fusion(bf16[12,2,2,120,2,120]{5,4,3,2,1,0:T(2,128)(2,1)S(1)} %get-tuple-element.213, s32[1024]{0:T(1024)S(1)} %pad_clamp_fusion.2), kind=kCustom, calls=%fused_computation.clone.1 | custom fusion | bytes 58982912 | tf_op jit(solution)/shard_map/while/body/eval_jaxpr/jit(_take)/gather | solution.py:120
  497.8 19.0 %fusion.92 = f32[120,4,2,16,1,2,2,8]{0,1,2,5,6,7,3,4:T(4,128)S(1)} fusion(bf16[8,16,2,2,120,2,120]{6,5,4,3,2,1,0:T(2,128)(2,1)} %bitcast.201, pred[8,16]{0,1:T(8,128)(4,1)S(1)} %copy.146, bf16[120,4,2,16,1,2,8]{0,6,5,3,2,1,4:T(8,128)(2,1)S(1)} %constant_dynamic-slice_fusion.2), kind=kOutput, calls=%fused_computation.6.clone.1 | convolution fusion | flops 250675200 | bytes 31948928 | tf_op jit(solution)/shard_map/while/body/eval_jaxpr/gjsxyad,dtajfqg->ytxjfsqg/dot_general | solution.py:121
  519.8 64.6 %gather_fusion = bf16[128,2,2,120,2,120]{5,4,3,2,1,0:T(2,128)(2,1)} fusion(bf16[12,2,2,120,2,120]{5,4,3,2,1,0:T(2,128)(2,1)S(1)} %get-tuple-element.213, s32[1024]{0:T(1024)S(1)} %pad_clamp_fusion.2), kind=kCustom, calls=%fused_computation.clone.1 | custom fusion | bytes 58982912 | tf_op jit(solution)/shard_map/while/body/eval_jaxpr/jit(_take)/gather | solution.py:120
  584.4 19.0 %fusion.92 = f32[120,4,2,16,1,2,2,8]{0,1,2,5,6,7,3,4:T(4,128)S(1)} fusion(bf16[8,16,2,2,120,2,120]{6,5,4,3,2,1,0:T(2,128)(2,1)} %bitcast.201, pred[8,16]{0,1:T(8,128)(4,1)S(1)} %copy.146, bf16[120,4,2,16,1,2,8]{0,6,5,3,2,1,4:T(8,128)(2,1)S(1)} %constant_dynamic-slice_fusion.2), kind=kOutput, calls=%fused_computation.6.clone.1 | convolution fusion | flops 250675200 | bytes 31948928 | tf_op jit(solution)/shard_map/while/body/eval_jaxpr/gjsxyad,dtajfqg->ytxjfsqg/dot_general | solution.py:121
  606.3 64.6 %gather_fusion = bf16[128,2,2,120,2,120]{5,4,3,2,1,0:T(2,128)(2,1)} fusion(bf16[12,2,2,120,2,120]{5,4,3,2,1,0:T(2,128)(2,1)S(1)} %get-tuple-element.213, s32[1024]{0:T(1024)S(1)} %pad_clamp_fusion.2), kind=kCustom, calls=%fused_computation.clone.1 | custom fusion | bytes 58982912 | tf_op jit(solution)/shard_map/while/body/eval_jaxpr/jit(_take)/gather | solution.py:120
  670.9 19.0 %fusion.92 = f32[120,4,2,16,1,2,2,8]{0,1,2,5,6,7,3,4:T(4,128)S(1)} fusion(bf16[8,16,2,2,120,2,120]{6,5,4,3,2,1,0:T(2,128)(2,1)} %bitcast.201, pred[8,16]{0,1:T(8,128)(4,1)S(1)} %copy.146, bf16[120,4,2,16,1,2,8]{0,6,5,3,2,1,4:T(8,128)(2,1)S(1)} %constant_dynamic-slice_fusion.2), kind=kOutput, calls=%fused_computation.6.clone.1 | convolution fusion | flops 250675200 | bytes 31948928 | tf_op jit(solution)/shard_map/while/body/eval_jaxpr/gjsxyad,dtajfqg->ytxjfsqg/dot_general | solution.py:121
  692.8 64.5 %gather_fusion = bf16[128,2,2,120,2,120]{5,4,3,2,1,0:T(2,128)(2,1)} fusion(bf16[12,2,2,120,2,120]{5,4,3,2,1,0:T(2,128)(2,1)S(1)} %get-tuple-element.213, s32[1024]{0:T(1024)S(1)} %pad_clamp_fusion.2), kind=kCustom, calls=%fused_computation.clone.1 | custom fusion | bytes 58982912 | tf_op jit(solution)/shard_map/while/body/eval_jaxpr/jit(_take)/gather | solution.py:120
  757.3 19.0 %fusion.92 = f32[120,4,2,16,1,2,2,8]{0,1,2,5,6,7,3,4:T(4,128)S(1)} fusion(bf16[8,16,2,2,120,2,120]{6,5,4,3,2,1,0:T(2,128)(2,1)} %bitcast.201, pred[8,16]{0,1:T(8,128)(4,1)S(1)} %copy.146, bf16[120,4,2,16,1,2,8]{0,6,5,3,2,1,4:T(8,128)(2,1)S(1)} %constant_dynamic-slice_fusion.2), kind=kOutput, calls=%fused_computation.6.clone.1 | convolution fusion | flops 250675200 | bytes 31948928 | tf_op jit(solution)/shard_map/while/body/eval_jaxpr/gjsxyad,dtajfqg->ytxjfsqg/dot_general | solution.py:121
  779.3 64.6 %gather_fusion = bf16[128,2,2,120,2,120]{5,4,3,2,1,0:T(2,128)(2,1)} fusion(bf16[12,2,2,120,2,120]{5,4,3,2,1,0:T(2,128)(2,1)S(1)} %get-tuple-element.213, s32[1024]{0:T(1024)S(1)} %pad_clamp_fusion.2), kind=kCustom, calls=%fused_computation.clone.1 | custom fusion | bytes 58982912 | tf_op jit(solution)/shard_map/while/body/eval_jaxpr/jit(_take)/gather | solution.py:120
  843.9 19.0 %fusion.92 = f32[120,4,2,16,1,2,2,8]{0,1,2,5,6,7,3,4:T(4,128)S(1)} fusion(bf16[8,16,2,2,120,2,120]{6,5,4,3,2,1,0:T(2,128)(2,1)} %bitcast.201, pred[8,16]{0,1:T(8,128)(4,1)S(1)} %copy.146, bf16[120,4,2,16,1,2,8]{0,6,5,3,2,1,4:T(8,128)(2,1)S(1)} %constant_dynamic-slice_fusion.2), kind=kOutput, calls=%fused_computation.6.clone.1 | convolution fusion | flops 250675200 | bytes 31948928 | tf_op jit(solution)/shard_map/while/body/eval_jaxpr/gjsxyad,dtajfqg->ytxjfsqg/dot_general | solution.py:121
  870.8 93.0 %all_to_all.10 = bf16[120,128,1,128]{3,0,2,1:T(8,128)(2,1)} all-to-all(bf16[120,128,1,128]{3,0,2,1:T(8,128)(2,1)} %copy.91), channel_id=1, replica_groups=mesh['groups'=2,'tm'=4,'chan'=2,'sub'=2] {'tm','chan'}, dimensions={1} | all-to-all | bytes 7864320 | tf_op jit(solution)/shard_map/all_to_all | solution.py:133
  980.2 8.5 copy.98
  (127 shorter events, 105.6 us)
Async XLA Ops:
  4.3 26.3 %collective-permute-start = (bf16[2,120,4096]{2,1,0:T(8,128)(2,1)}, bf16[2,120,4096]{2,1,0:T(8,128)(2,1)}, u32[]{:S(2)}, u32[]{:S(2)}) collective-permute-start(bf16[2,120,4096]{2,1,0:T(8,128)(2,1)} %broadcast_multiply_fusion), channel_id=1, source_target_pairs={{0,1},{1,4},{4,5},{5,8},{8,9},{9,12},{12,13},{2,3},{3,6},{6,7},{7,... | collective-permute-start | bytes 5898248 | tf_op jit(solution)/shard_map/ppermute | solution.py:17
  17.2 30.2 %copy-start = (f32[128,64]{0,1:T(8,128)}, f32[128,64]{0,1:T(8,128)S(1)}, u32[]{:S(2)}) copy-start(f32[128,64]{0,1:T(8,128)S(1)} %get-tuple-element.152) | copy-start | bytes 98308
  17.3 30.2 %copy-start.2 = (f32[128,64]{0,1:T(8,128)}, f32[128,64]{0,1:T(8,128)S(1)}, u32[]{:S(2)}) copy-start(f32[128,64]{0,1:T(8,128)S(1)} %get-tuple-element.153) | copy-start | bytes 98308
  48.5 1.2 copy-start.9
  74.1 6.3 copy-start.8
  74.1 88.9 %all-to-all-start = ((bf16[120,128,1,128]{3,0,2,1:T(8,128)(2,1)}), bf16[120,128,1,128]{3,0,2,1:T(8,128)(2,1)}, u32[]{:S(2)}, u32[]{:S(2)}) async-start(bf16[120,128,1,128]{3,0,2,1:T(8,128)(2,1)} %copy.86), calls=%async_computation | async-start | bytes 7864320 | tf_op jit(solution)/shard_map/all_to_all | solution.py:106
  963.8 6.7 copy-start.6
  963.8 6.7 copy-start.7
  970.5 3.4 copy-start.1
  970.5 3.4 copy-start.3
  974.9 1.0 copy-start.4
  974.9 1.0 copy-start.5
  980.2 8.5 copy-start.10
where the time goes:
time: 999 us; the launch traced here: 994 us
  local copies, waits for them, and re-layouts  601 us (60%)
  matrix products  166 us (17%)
  blocking collectives  93 us (9%)
  waiting for transfers between devices  87.8 us (9%)
  other arithmetic  37.1 us (4%)
    gather x8, local copies, waits for them, and re-layouts, equalise_group(): chosen = jnp.take(shaped_weights, picks, axis=0)  517 us
    dot_general x8, matrix products, equalise_group(): jnp.einsum('gjsxyad,dtajfqg->ytxjfsqg', chosen, columns, preferred_elemen...  152 us
    all_to_all x1, blocking collectives, on_device(): lax.all_to_all(equalised.reshape(channels_dev, N1, frame_count, 2 * N2),...  93 us
    all_to_all x1, waiting for transfers between devices, on_device(): lax.all_to_all(dispersed, ('tm', 'chan'), split_axis=1, concat_axis=1, ti...  76.2 us
  transfers between devices with their start and end apart: 2, of which 2 were waited for; matrix products, arithmetic and copies ran while one was open for 2% of the time, Pallas kernels for 0%

commit v1 on v0

--- a/solution.py
+++ b/solution.py
@@ -1,14 +1,20 @@
+import functools
 import math
 
 import jax
 import jax.numpy as jnp
 from jax import lax
+from jax.experimental import pallas as pl
+from jax.experimental.pallas import tpu as pltpu
 from jax.sharding import PartitionSpec as P
 
 TAPS = 4096
 N1 = 128
 NFFT = 8192
 N2 = 64
+LANES = 2 * N2
+BLOCK = 8
+QUARTERS = 4
 
 
 def from_behind(value, axis, by):
@@ -17,13 +23,16 @@
     return lax.ppermute(value, axis, pairs)
 
 
+def cos_sin(rows, columns, length):
+    product = rows[:, None] * columns[None, :] % length
+    angle = product.astype(jnp.float32) * (2.0 * math.pi / length)
+    factor = 1.0 / math.sqrt(length)
+    return jnp.cos(angle) * factor, jnp.sin(angle) * factor
+
+
 def dft_table(length, inverse):
     counter = jnp.arange(length, dtype=jnp.int32)
-    product = counter[:, None] * counter[None, :] % length
-    angle = product.astype(jnp.float32) * (2.0 * math.pi / length)
-    factor = 1.0 / math.sqrt(length)
-    cosine = jnp.cos(angle) * factor
-    sine = jnp.sin(angle) * factor
+    cosine, sine = cos_sin(counter, counter, length)
     if inverse:
         upper = jnp.stack([cosine, -sine], axis=1)
         lower = jnp.stack([sine, cosine], axis=1)
@@ -38,6 +47,395 @@
     product = first_rows[:, None] * seconds[None, :] % NFFT
     angle = product.astype(jnp.float32) * (2.0 * math.pi / NFFT)
     return (jnp.cos(angle), jnp.sin(angle))
+
+
+def low_half():
+    return lax.broadcasted_iota(jnp.int32, (BLOCK, LANES), 1) < N2
+
+
+def swap_halves(value):
+    return pltpu.roll(value, N2, 1)
+
+
+def forward_kernel(
+    tail, own, first, twist_cos, twist_sin, second, chirp, *refs, slots, rows
+):
+    outs, (spread, mixed) = refs[:slots], refs[slots:]
+    low = low_half()
+    half_tiles = TAPS // LANES
+    for tile in range(2 * half_tiles):
+        source = tail if tile < half_tiles else own
+        at = (tile % half_tiles) * LANES
+        real = source[0, :, at : at + LANES].astype(jnp.float32)
+        imag = source[1, :, at : at + LANES].astype(jnp.float32)
+        real_r = swap_halves(real)
+        imag_r = swap_halves(imag)
+        even = 2 * tile
+        spread[pl.ds(even, BLOCK, stride=2 * N1), :] = jnp.where(low, real, imag_r)
+        spread[pl.ds(even + 1, BLOCK, stride=2 * N1), :] = jnp.where(low, real_r, imag)
+        spread[pl.ds(N1 + even, BLOCK, stride=2 * N1), :] = jnp.where(low, imag, -real_r)
+        spread[pl.ds(N1 + even + 1, BLOCK, stride=2 * N1), :] = jnp.where(low, imag_r, -real)
+    table = first[...]
+    cosine = twist_cos[...]
+    sine = twist_sin[...]
+    count = slots * rows
+    for pair in range(BLOCK // 2):
+        at = 4 * N1 * pair
+        both = jnp.concatenate(
+            [
+                spread[at : at + 2 * N1, :].astype(jnp.bfloat16),
+                spread[at + 2 * N1 : at + 4 * N1, :].astype(jnp.bfloat16),
+            ],
+            axis=1,
+        )
+        section = jnp.dot(table, both, preferred_element_type=jnp.float32)
+        for side in range(2):
+            part = section[:, side * LANES : (side + 1) * LANES]
+            part = part * cosine + swap_halves(part) * sine
+            mixed[pl.ds(2 * pair + side, count, stride=BLOCK), :] = part
+    spectrum = jnp.dot(
+        mixed[...].astype(jnp.bfloat16), second[...], preferred_element_type=jnp.float32
+    )
+    step_c = chirp[4 * slots]
+    step_s = chirp[4 * slots + 1]
+    for slot in range(slots):
+        turn_c, turn_s, move_c, move_s = (chirp[4 * slot + i] for i in range(4))
+        for row in range(rows):
+            at = (slot * rows + row) * BLOCK
+            part = spectrum[at : at + BLOCK]
+            part = part * turn_c + swap_halves(part) * turn_s
+            outs[slot][row] = part.astype(jnp.bfloat16)
+            if row + 1 < rows:
+                turn_c, turn_s = (
+                    turn_c * move_c - turn_s * move_s,
+                    turn_s * move_c + turn_c * move_s,
+                )
+                move_c, move_s = (
+                    move_c * step_c - move_s * step_s,
+                    move_s * step_c + move_c * step_s,
+                )
+
+
+def forward(tail, own, tables, chirp, slots, rows):
+    channels = own.shape[1]
+    first, twist_cos, twist_sin, second = tables
+    whole = lambda a: pl.BlockSpec(a.shape, lambda i: (0,) * a.ndim)
+    samples = pl.BlockSpec((2, BLOCK, TAPS), lambda i: (0, i, 0))
+    return pl.pallas_call(
+        functools.partial(forward_kernel, slots=slots, rows=rows),
+        grid=(channels // BLOCK,),
+        in_specs=[
+            samples,
+            samples,
+            whole(first),
+            whole(twist_cos),
+            whole(twist_sin),
+            whole(second),
+            pl.BlockSpec((chirp.shape[0], BLOCK, LANES), lambda i: (0, i, 0)),
+        ],
+        out_specs=[pl.BlockSpec((rows, BLOCK, LANES), lambda i: (0, i, 0))] * slots,
+        out_shape=[jax.ShapeDtypeStruct((rows, channels, LANES), jnp.bfloat16)] * slots,
+        scratch_shapes=[
+            pltpu.VMEM((BLOCK * 2 * N1, LANES), jnp.float32),
+            pltpu.VMEM((slots * rows * BLOCK, LANES), jnp.float32),
+        ],
+        name="forward",
+    )(tail, own, first, twist_cos, twist_sin, second, chirp)
+
+
+def equalise_kernel(
+    scalars, w0, w1, w2, w3, picks, near, far, second, turn_cos, turn_sin, keep, send,
+    columns, total, *, blocks, channels
+):
+    first_side = scalars[0] == 0
+    quarter = scalars[1]
+    per = blocks // QUARTERS
+    all_channels = 2 * channels
+    for side in range(2):
+        mine = near[side].astype(jnp.float32)
+        other = far[side].astype(jnp.float32)
+        lanes = slice(side * LANES, (side + 1) * LANES)
+        columns[0:channels, lanes] = jnp.where(first_side, mine, other)
+        columns[channels:all_channels, lanes] = jnp.where(first_side, other, mine)
+    value = columns[...].astype(jnp.bfloat16)
+    pair = pl.program_id(0)
+    table = picks[:, 0:LANES].astype(jnp.float32)
+    index = lax.broadcasted_iota(jnp.int32, table.shape, 0)
+    chosen = jnp.concatenate(
+        [
+            jnp.sum(jnp.where(index == 2 * pair + side, table, 0.0), axis=0, keepdims=True)
+            for side in range(2)
+        ],
+        axis=1,
+    )
+    for place in range(QUARTERS):
+        weights = (w0, w1, w2, w3)[place]
+        owner = jnp.bitwise_xor(quarter, place)
+        for item in range(per):
+            name = (owner * per + item).astype(jnp.float32)
+            mask = jnp.where(chosen == name, 1.0, 0.0).astype(jnp.bfloat16)
+            block = weights[item * 2 * all_channels : (item + 1) * 2 * all_channels, :]
+            product = jnp.dot(block, value * mask, preferred_element_type=jnp.float32)
+            if place == 0 and item == 0:
+                total[...] = product
+            else:
+                total[...] += product
+    low = lax.broadcasted_iota(jnp.int32, (1, LANES), 1) < N2
+    sign = jnp.where(low, -1.0, 1.0)
+    table = second[...]
+    for side in range(2):
+        lanes = slice(side * LANES, (side + 1) * LANES)
+        mixed = total[0:all_channels, lanes] + sign * swap_halves(
+            total[all_channels : 2 * all_channels, lanes]
+        )
+        partial = jnp.dot(
+            mixed.astype(jnp.bfloat16), table, preferred_element_type=jnp.float32
+        )
+        turned = partial * turn_cos[side] + swap_halves(partial) * turn_sin[side]
+        lower = turned[0:channels]
+        upper = turned[channels:all_channels]
+        keep[side] = jnp.where(first_side, lower, upper).astype(jnp.bfloat16)
+        send[side] = jnp.where(first_side, upper, lower).astype(jnp.bfloat16)
+
+
+def equalise(scalars, weights, places, picks, picks_at, near, far, second, turn_cos, turn_sin, blocks):
+    rows, channels, _ = near.shape
+    per = blocks // QUARTERS
+    height = per * 4 * channels
+    width = 2 * channels
+    pairs = pl.BlockSpec((2, channels, LANES), lambda i, s: (i, 0, 0))
+    turn = pl.BlockSpec((2, 1, LANES), lambda i, s: (i, 0, 0))
+    fixed = pl.Buffered(1)
+    return pl.pallas_call(
+        functools.partial(equalise_kernel, blocks=blocks, channels=channels),
+        grid_spec=pltpu.PrefetchScalarGridSpec(
+            num_scalar_prefetch=1,
+            grid=(rows // 2,),
+            in_specs=[
+                pl.BlockSpec((height, width), lambda i, s, j=j: (j, 0), pipeline_mode=fixed)
+                for j in places
+            ]
+            + [
+                pl.BlockSpec((rows, width), lambda i, s: (picks_at, 0), pipeline_mode=fixed),
+                pairs,
+                pairs,
+                pl.BlockSpec((LANES, LANES), lambda i, s: (0, 0)),
+                turn,
+                turn,
+            ],
+            out_specs=[pairs, pairs],
+            scratch_shapes=[
+                pltpu.VMEM((2 * channels, 2 * LANES), jnp.float32),
+                pltpu.VMEM((4 * channels, 2 * LANES), jnp.float32),
+            ],
+        ),
+        out_shape=[jax.ShapeDtypeStruct(near.shape, jnp.bfloat16)] * 2,
+        name="equalise",
+    )(scalars, *weights, picks, near, far, second, turn_cos, turn_sin)
+
+
+def backward_kernel(*refs, parts, rows):
+    ins, (last, mask, out, spread, mixed) = refs[:parts], refs[parts:]
+    low = low_half()
+    for part in range(parts):
+        for row in range(rows):
+            value = ins[part][row].astype(jnp.float32)
+            at = part * rows + row
+            spread[pl.ds(at, BLOCK, stride=2 * N1), :] = value
+            turned = swap_halves(value)
+            spread[pl.ds(N1 + at, BLOCK, stride=2 * N1), :] = jnp.where(low, -turned, turned)
+    table = last[...]
+    half = N1 // 2
+    for pair in range(BLOCK // 2):
+        at = 4 * N1 * pair
+        both = jnp.concatenate(
+            [
+                spread[at : at + 2 * N1, :].astype(jnp.bfloat16),
+                spread[at + 2 * N1 : at + 4 * N1, :].astype(jnp.bfloat16),
+            ],
+            axis=1,
+        )
+        value = jnp.dot(table, both, preferred_element_type=jnp.float32)
+        for side in range(2):
+            mixed[pl.ds(2 * pair + side, half, stride=BLOCK), :] = value[
+                :, side * LANES : (side + 1) * LANES
+            ]
+    scale = mask[...]
+    for tile in range(half // 2):
+        even = mixed[2 * tile * BLOCK : (2 * tile + 1) * BLOCK, :]
+        odd = mixed[(2 * tile + 1) * BLOCK : (2 * tile + 2) * BLOCK, :]
+        at = slice(tile * LANES, (tile + 1) * LANES)
+        real = jnp.where(low, even, swap_halves(odd)) * scale
+        imag = jnp.where(low, swap_halves(even), odd) * scale
+        out[0, :, at] = real.astype(jnp.bfloat16)
+        out[1, :, at] = imag.astype(jnp.bfloat16)
+
+
+def backward(parts, last, mask):
+    rows, channels, _ = parts[0].shape
+    return pl.pallas_call(
+        functools.partial(backward_kernel, parts=len(parts), rows=rows),
+        grid=(channels // BLOCK,),
+        in_specs=[pl.BlockSpec((rows, BLOCK, LANES), lambda i: (0, i, 0))] * len(parts)
+        + [
+            pl.BlockSpec(last.shape, lambda i: (0, 0)),
+            pl.BlockSpec((BLOCK, LANES), lambda i: (i, 0)),
+        ],
+        out_specs=pl.BlockSpec((2, BLOCK, TAPS), lambda i: (0, i, 0)),
+        out_shape=jax.ShapeDtypeStruct((2, channels, TAPS), jnp.bfloat16),
+        scratch_shapes=[
+            pltpu.VMEM((BLOCK * 2 * N1, LANES), jnp.float32),
+            pltpu.VMEM((N1 // 2 * BLOCK, LANES), jnp.float32),
+        ],
+        name="backward",
+    )(*parts, last, mask)
+
+
+def both(value):
+    return jnp.concatenate([value, value], axis=-1)
+
+
+def signed(value, first):
+    return jnp.concatenate([first * value, -first * value], axis=-1)
+
+
+def chirp_table(dispersion, mask, bases, rows):
+    seconds = jnp.arange(N2, dtype=jnp.int32)
+    base = bases[:, None] + N1 * seconds[None, :]
+    centred = jnp.where(base < NFFT // 2, base, base - NFFT)
+    whole = float(NFFT * NFFT)
+    start = (centred * centred).astype(jnp.float32) / whole
+    quarter = jnp.mod(centred, 4).astype(jnp.float32) * (0.5 * math.pi)
+    change = (2 * centred + 1).astype(jnp.float32) / whole
+    phase = dispersion[None, :, None] * start[:, None] - quarter[:, None]
+    move = dispersion[None, :, None] * change[:, None] - 0.5 * math.pi
+    scale = mask[None, :, None]
+    slots = jnp.stack(
+        [
+            both(jnp.cos(phase) * scale),
+            signed(jnp.sin(phase) * scale, -1.0),
+            both(jnp.cos(move)),
+            signed(jnp.sin(move), -1.0),
+        ],
+        axis=1,
+    )
+    step = jnp.broadcast_to(dispersion[:, None] * (2.0 / whole), (dispersion.shape[0], N2))
+    step = jnp.stack([both(jnp.cos(step)), signed(jnp.sin(step), -1.0)])
+    return jnp.concatenate([slots.reshape((-1,) + slots.shape[2:]), step])
+
+
+def second_table(inverse):
+    counter = jnp.arange(N2, dtype=jnp.int32)
+    cosine, sine = cos_sin(counter, counter, N2)
+    sine = -sine if inverse else sine
+    upper = jnp.concatenate([cosine, -sine], axis=1)
+    lower = jnp.concatenate([sine, cosine], axis=1)
+    return jnp.concatenate([upper, lower], axis=0).astype(jnp.bfloat16)
+
+
+def near_blocks(signal, channel_mask, dispersion, equaliser, bin_block):
+    channels = signal.shape[1]
+    blocks = equaliser.shape[0]
+    tm = lax.axis_size("tm")
+    chan = lax.axis_size("chan")
+    subs = lax.axis_size("sub")
+    rows = N1 // (tm * chan)
+    z = lax.axis_index("tm")
+    x = lax.axis_index("chan")
+    quarter = lax.axis_index("groups") * subs + lax.axis_index("sub")
+    per = blocks // QUARTERS
+    width = 2 * channels
+
+    tail = from_behind(signal, ("tm", "sub"), 1)
+
+    picks = jnp.transpose(bin_block).astype(jnp.bfloat16)
+    picks = jnp.concatenate(
+        [picks, picks, jnp.zeros((rows, width - LANES), jnp.bfloat16)], axis=1
+    )
+    own_part = lax.dynamic_slice_in_dim(equaliser, quarter * per, per, 0)
+    own_part = jnp.concatenate([own_part.reshape(per * 2 * width, width), picks], axis=0)
+    swap = [(0, 1), (1, 0)]
+    weights = {0: [equaliser.reshape(blocks * 2 * width, width)] * QUARTERS}
+    for step in (1, tm - 1, *range(2, tm - 1)):
+        got = lax.ppermute(own_part, "tm", [(i, (i + step) % tm) for i in range(tm)])
+        across = lax.ppermute(got, "groups", swap)
+        weights[step] = [
+            got,
+            lax.ppermute(got, "sub", swap),
+            across,
+            lax.ppermute(across, "sub", swap),
+        ]
+    order = [0, 1, tm - 1, *range(2, tm - 1)]
+    row = jnp.arange(rows, dtype=jnp.int32)
+    bases = jnp.mod(z - jnp.array(order, jnp.int32), tm) * chan
+    own_bases = (bases + x) * rows
+    other_bases = (bases + (1 - x)) * rows
+    own_rows = (own_bases[:, None] + row[None]).reshape(-1)
+    other_rows = (other_bases[:, None] + row[None]).reshape(-1)
+
+    firsts = jnp.arange(N1, dtype=jnp.int32)
+    second = second_table(False)
+
+    def forward_tables(k1):
+        table = jnp.concatenate(cos_sin(k1, firsts, N1), axis=1).astype(jnp.bfloat16)
+        cosine, sine = twist_table(k1, N2)
+        return table, both(cosine), signed(sine, 1.0), second
+
+    mask = channel_mask.astype(jnp.float32)
+    send = forward(
+        tail, signal, forward_tables(other_rows),
+        chirp_table(dispersion, mask, other_bases, rows), tm, rows,
+    )
+    keep = forward(
+        tail, signal, forward_tables(own_rows),
+        chirp_table(dispersion, mask, own_bases, rows), tm, rows,
+    )
+    got = [lax.ppermute(part, "chan", swap) for part in send]
+
+    inverse = second_table(True)
+    cosine, sine = twist_table(own_rows, N2)
+    turn_cos = both(cosine).reshape(tm, rows, 1, LANES)
+    turn_sin = signed(sine, -1.0).reshape(tm, rows, 1, LANES)
+    mine, theirs = [], []
+    for slot, step in enumerate(order):
+        local = step == 0
+        scalars = jnp.stack([x, jnp.zeros_like(quarter) if local else quarter])
+        kept, sent = equalise(
+            scalars,
+            weights[step],
+            range(QUARTERS) if local else [0] * QUARTERS,
+            picks if local else weights[step][0],
+            0 if local else per * 2 * width // rows,
+            keep[slot],
+            got[slot],
+            inverse,
+            turn_cos[slot],
+            turn_sin[slot],
+            blocks,
+        )
+        mine.append(kept)
+        theirs.append(lax.ppermute(sent, "chan", swap))
+
+    last = jnp.concatenate(
+        cos_sin(firsts[N1 // 2 :], jnp.concatenate([own_rows, other_rows]), N1), axis=1
+    ).astype(jnp.bfloat16)
+    spread_mask = jnp.broadcast_to(mask[:, None], (channels, LANES))
+    return backward(mine + theirs, last, spread_mask)
+
+
+def invert_second(spectra, first_rows, inverse_second):
+    partial_value = jnp.einsum(
+        "rspk,cjfpk->cjfrs", inverse_second, spectra, preferred_element_type=jnp.float32
+    )
+    cos_inv, sin_inv = twist_table(first_rows, N2)
+    cos_inv = cos_inv[:, None, :]
+    sin_inv = sin_inv[:, None, :]
+    real_g = partial_value[:, :, :, 0]
+    imag_g = partial_value[:, :, :, 1]
+    turned = jnp.stack(
+        [real_g * cos_inv - imag_g * sin_inv, imag_g * cos_inv + real_g * sin_inv], axis=3
+    )
+    return turned.astype(jnp.bfloat16)
 
 
 def phase_table(dispersion):
@@ -51,22 +449,7 @@
     return (jnp.cos(phase), jnp.sin(phase))
 
 
-def invert_second(spectra, first_rows, inverse_second):
-    partial_value = jnp.einsum(
-        "rspk,cjfpk->cjfrs", inverse_second, spectra, preferred_element_type=jnp.float32
-    )
-    cos_inv, sin_inv = twist_table(first_rows, N2)
-    cos_inv = cos_inv[:, None, :]
-    sin_inv = sin_inv[:, None, :]
-    real_g = partial_value[:, :, :, 0]
-    imag_g = partial_value[:, :, :, 1]
-    turned = jnp.stack(
-        [real_g * cos_inv - imag_g * sin_inv, imag_g * cos_inv + real_g * sin_inv], axis=3
-    )
-    return turned.astype(jnp.bfloat16)
-
-
-def on_device(signal, channel_mask, dispersion, equaliser, bin_block):
+def far_blocks(signal, channel_mask, dispersion, equaliser, bin_block):
     channels_dev = signal.shape[1]
     frame_count = signal.shape[2] // TAPS
     half_rows = N1 // 2
@@ -149,6 +532,24 @@
     return (values * channel_mask.astype(jnp.float32)[None, :, None]).astype(jnp.bfloat16)
 
 
+def on_device(signal, channel_mask, dispersion, equaliser, bin_block):
+    tm = lax.axis_size("tm")
+    chan = lax.axis_size("chan")
+    sharers = lax.axis_size("groups") * lax.axis_size("sub")
+    rows = N1 // (tm * chan)
+    fits = (
+        chan == 2
+        and 2 <= tm <= 4
+        and sharers == QUARTERS
+        and equaliser.shape[0] % QUARTERS == 0
+        and rows % 16 == 0
+        and signal.shape[2] == TAPS
+        and signal.shape[1] % BLOCK == 0
+    )
+    plan = near_blocks if fits else far_blocks
+    return plan(signal, channel_mask, dispersion, equaliser, bin_block)
+
+
 def solution(mesh):
     in_specs = (
         P(None, "chan", ("groups", "tm", "sub")),

time: 999 us -> 282 us (0.28)
  local copies, waits for them, and re-layouts: 601 us -> 33.5 us
  matrix products: 166 us -> 0 us
  Pallas kernels: 0 us -> 120 us
  blocking collectives: 93 us -> 0 us
  other arithmetic: 37.1 us -> 18.9 us
    gather x8 -> x0, local copies, waits for them, and re-layouts: 517 us -> none  [equalise_group(): chosen = jnp.take(shaped_weights, picks, axis=0)]
    dot_general x12 -> x0, matrix products: 166 us -> none  [the longest x8 152 us: equalise_group(): jnp.einsum('gjsxyad,dtajfqg->ytxjfsqg', chosen, columns, preferred_elemen...]
    pallas_call x0 -> x7, Pallas kernels: none -> 120 us  [the longest x4 57 us: equalise(): pl.pallas_call(functools.partial(equalise_kernel, blocks=blocks, channels...]
    all_to_all x1 -> x0, blocking collectives: 93 us -> none  [on_device(): lax.all_to_all(equalised.reshape(channels_dev, N1, frame_count, 2 * N2),...]
    ppermute x0 -> x20, waiting for transfers between devices: none -> 91.2 us  [the longest x3 47.3 us: near_blocks(): lax.ppermute(own_part, 'tm', [(i, (i + step) % tm) for i in range(tm)])]
    all_to_all x1 -> x0, waiting for transfers between devices: 76.2 us -> none  [on_device(): lax.all_to_all(dispersed, ('tm', 'chan'), split_axis=1, concat_axis=1, ti...]
    another operation x36 -> x14, other arithmetic: 29.9 us -> 5.54 us  [the longest x6 3.18 us: chirp_table(): jnp.stack([both(jnp.cos(phase) * scale), signed(jnp.sin(phase) * scale, -...]
    ppermute x1 -> x12, local copies, waits for them, and re-layouts: 3.11 us -> 26.1 us  [the longest x3 6.83 us: near_blocks(): lax.ppermute(got, 'sub', swap)]
  transfers between devices with their start and end apart: 2 -> 21, of which waited for: 2 -> 6; matrix products, arithmetic and copies ran while one was open for 2% -> 16% of each run, Pallas kernels for 0% -> 37%
where the time goes in v1:
time: 282 us; the launch traced here: 281 us
  Pallas kernels  120 us (43%)
  waiting for transfers between devices  91.2 us (32%)
  local copies, waits for them, and re-layouts  33.5 us (12%)
  other arithmetic  18.9 us (7%)
  starting transfers between devices  17.6 us (6%)
    pallas_call x4, Pallas kernels, equalise(): pl.pallas_call(functools.partial(equalise_kernel, blocks=blocks, channels...  57 us
    ppermute x3, waiting for transfers between devices, near_blocks(): lax.ppermute(own_part, 'tm', [(i, (i + step) % tm) for i in range(tm)])  47.3 us
    pallas_call x2, Pallas kernels, forward(): pl.pallas_call(functools.partial(forward_kernel, slots=slots, rows=rows),...  46 us
    ppermute x3, waiting for transfers between devices, near_blocks(): across = lax.ppermute(got, 'groups', swap)  34.1 us
    pallas_call x1, Pallas kernels, backward(): pl.pallas_call(functools.partial(backward_kernel, parts=len(parts), rows=...  16.8 us
    ppermute x4, waiting for transfers between devices, near_blocks(): theirs.append(lax.ppermute(sent, 'chan', swap))  9.84 us
    ppermute x3, local copies, waits for them, and re-layouts, near_blocks(): lax.ppermute(got, 'sub', swap)  6.83 us
    ppermute x3, local copies, waits for them, and re-layouts, near_blocks(): across = lax.ppermute(got, 'groups', swap)  6.83 us
  transfers between devices with their start and end apart: 21, of which 6 were waited for; matrix products, arithmetic and copies ran while one was open for 16% of the time, Pallas kernels for 37%

profile of v1, /device:TPU:20, one launch (start us, length us, event | category | flops | bytes accessed | tf_op | source)
XLA Modules:
  0.0 281.3 jit_solution(17111072656597156454)
XLA Ops:
  10.0 4.6 %cosine_multiply_fusion = (f32[4,120,64]{2,1,0:T(8,128)S(1)}, f32[4,120,64]{2,1,0:T(8,128)S(1)}, f32[4,120,64]{2,1,0:T(8,128)}, f32[4,120,64]{2,1,0:T(8,128)S(1)...) fusion(f32[4,64]{1,0:T(4,128)S(1)} %get-tuple-element.70, ...), kind=kLoop, calls=%fused_computation.19 | loop fusion | flops 491520 | bytes 1481664 | tf_op jit(solution)/shard_map/mul | solution.py:315
  18.9 35.8 %collective-permute-done.2 = bf16[1456,240]{0,1:T(8,128)(2,1)} collective-permute-done((bf16[1456,240]{0,1:T(8,128)(2,1)}, bf16[1456,240]{0,1:T(8,128)(2,1)}, u32[]{:S(2)}, u32[]{:S(2)}) %collective-permute-start.2) | collective-permute-done | bytes 698912 | tf_op jit(solution)/shard_map/ppermute | solution.py:360
  56.8 11.4 %collective-permute-done.12 = bf16[1456,240]{0,1:T(8,128)(2,1)} collective-permute-done((bf16[1456,240]{0,1:T(8,128)(2,1)}, bf16[1456,240]{0,1:T(8,128)(2,1)}, u32[]{:S(2)}, u32[]{:S(2)}) %collective-permute-start.12) | collective-permute-done | bytes 698912 | tf_op jit(solution)/shard_map/ppermute | solution.py:360
  71.4 3.0 %collective-permute-done.4 = bf16[1456,240]{0,1:T(8,128)(2,1)} collective-permute-done((bf16[1456,240]{0,1:T(8,128)(2,1)}, bf16[1456,240]{0,1:T(8,128)(2,1)}, u32[]{:S(2)}, u32[]{:S(2)}) %collective-permute-start.4) | collective-permute-done | bytes 698912 | tf_op jit(solution)/shard_map/ppermute | solution.py:361
  74.4 15.8 %collective-permute-done.9 = bf16[1456,240]{0,1:T(8,128)(2,1)} collective-permute-done((bf16[1456,240]{0,1:T(8,128)(2,1)}, bf16[1456,240]{0,1:T(8,128)(2,1)}, u32[]{:S(2)}, u32[]{:S(2)}) %collective-permute-start.9) | collective-permute-done | bytes 698912 | tf_op jit(solution)/shard_map/ppermute | solution.py:361
  90.2 15.3 %collective-permute-done.14 = bf16[1456,240]{0,1:T(8,128)(2,1)} collective-permute-done((bf16[1456,240]{0,1:T(8,128)(2,1)}, bf16[1456,240]{0,1:T(8,128)(2,1)}, u32[]{:S(2)}, u32[]{:S(2)}) %collective-permute-start.14) | collective-permute-done | bytes 698912 | tf_op jit(solution)/shard_map/ppermute | solution.py:361
  109.8 23.0 %forward.3 = (bf16[16,120,128]{2,1,0:T(8,128)(2,1)}, bf16[16,120,128]{2,1,0:T(8,128)(2,1)}, bf16[16,120,128]{2,1,0:T(8,128)(2,1)}, bf16[16,120,128]{2,1,0:T(8,128)(2,1)}) custom-call(bf16[2,120,4096]{2,1,0:T(8,128)(2,1)} %collective-permute-done.tail, bf16[2,120,4096]{2,1,0:T(8,128)(2,1)} %own.3, bf16[64,256]{1,0:T(8,128)(2,1)} %pad_maximum_fusion.13.first, ...), custom_call_target="tpu_custom_call" | custom-call | tf_op jit(solution)/shard_map/forward/pallas_call | solution.py:124
  139.2 2.3 copy.26.w0.picks
  141.5 2.3 copy.33.w0.picks
  143.8 2.3 copy.40.w0.picks
  146.0 2.3 copy.28.w2
  148.3 2.2 copy.35.w2
  150.6 2.3 copy.42.w2
  155.1 2.3 copy.34.w1
  157.4 2.3 copy.41.w1
  159.7 23.0 %forward.2 = (bf16[16,120,128]{2,1,0:T(8,128)(2,1)}, bf16[16,120,128]{2,1,0:T(8,128)(2,1)}, bf16[16,120,128]{2,1,0:T(8,128)(2,1)}, bf16[16,120,128]{2,1,0:T(8,128)(2,1)}) custom-call(bf16[2,120,4096]{2,1,0:T(8,128)(2,1)} %collective-permute-done.tail, bf16[2,120,4096]{2,1,0:T(8,128)(2,1)} %own.3, bf16[64,256]{1,0:T(8,128)(2,1)} %pad_maximum_fusion.11.first, ...), custom_call_target="tpu_custom_call" | custom-call | tf_op jit(solution)/shard_map/forward/pallas_call | solution.py:124
  182.7 2.3 copy.29.w3
  184.9 2.3 copy.36.w3
  189.2 14.2 %equalise.4 = (bf16[16,120,128]{2,1,0:T(8,128)(2,1)}, bf16[16,120,128]{2,1,0:T(8,128)(2,1)}) custom-call(s32[2]{0:T(128)} %pad_add_fusion.scalars, bf16[5760,240]{1,0:T(8,128)(2,1)} %bitcast.56, bf16[5760,240]{1,0:T(8,128)(2,1)} %bitcast.57, bf16[5760,240]{1,0:T(8,128)(2,1)} %bitcast.58, bf16[5760,240]{1,0:T(8,128)(2,1)} %bitcast.59, ...), custom_call_target="tpu_custom_call" | custom-call | tf_op jit(solution)/shard_map/equalise/pallas_call | solution.py:209
  205.7 14.2 %equalise.5 = (bf16[16,120,128]{2,1,0:T(8,128)(2,1)}, bf16[16,120,128]{2,1,0:T(8,128)(2,1)}) custom-call(s32[2]{0:T(128)} %pad_add_fusion.1.scalars, bf16[1456,240]{1,0:T(8,128)(2,1)} %copy.26.w0.picks, bf16[1456,240]{1,0:T(8,128)(2,1)} %copy.27.w1, bf16[1456,240]{1,0:T(8,128)(2,1)} %copy.28.w2, bf16[1456,240]{1,0:T(8,128)(2,1)} %copy.29.w3, ...), custom_call_target="tpu_custom_call" | custom-call | tf_op jit(solution)/shard_map/equalise/pallas_call | solution.py:209
  221.3 14.4 %equalise.6 = (bf16[16,120,128]{2,1,0:T(8,128)(2,1)}, bf16[16,120,128]{2,1,0:T(8,128)(2,1)}) custom-call(s32[2]{0:T(128)} %pad_add_fusion.1.scalars, bf16[1456,240]{1,0:T(8,128)(2,1)} %copy.33.w0.picks, bf16[1456,240]{1,0:T(8,128)(2,1)} %copy.34.w1, bf16[1456,240]{1,0:T(8,128)(2,1)} %copy.35.w2, bf16[1456,240]{1,0:T(8,128)(2,1)} %copy.36.w3, ...), custom_call_target="tpu_custom_call" | custom-call | tf_op jit(solution)/shard_map/equalise/pallas_call | solution.py:209
  238.0 14.2 %equalise.7 = (bf16[16,120,128]{2,1,0:T(8,128)(2,1)}, bf16[16,120,128]{2,1,0:T(8,128)(2,1)}) custom-call(s32[2]{0:T(128)} %pad_add_fusion.1.scalars, bf16[1456,240]{1,0:T(8,128)(2,1)} %copy.40.w0.picks, bf16[1456,240]{1,0:T(8,128)(2,1)} %copy.41.w1, bf16[1456,240]{1,0:T(8,128)(2,1)} %copy.42.w2, bf16[1456,240]{1,0:T(8,128)(2,1)} %copy.43.w3, ...), custom_call_target="tpu_custom_call" | custom-call | tf_op jit(solution)/shard_map/equalise/pallas_call | solution.py:209
  253.9 9.8 %collective-permute-done.20.refs_7_ = bf16[16,120,128]{2,1,0:T(8,128)(2,1)S(1)} collective-permute-done((bf16[16,120,128]{2,1,0:T(8,128)(2,1)}, bf16[16,120,128]{2,1,0:T(8,128)(2,1)S(1)}, u32[]{:S(2)}, u32[]{:S(2)}) %collective-permute-start.20) | collective-permute-done | bytes 491552 | tf_op jit(solution)/shard_map/ppermute | solution.py:417
  264.5 16.8 %backward.1 = bf16[2,120,4096]{2,1,0:T(8,128)(2,1)} custom-call(bf16[16,120,128]{2,1,0:T(8,128)(2,1)} %get-tuple-element.23.refs_0_, bf16[16,120,128]{2,1,0:T(8,128)(2,1)} %get-tuple-element.26.refs_1_, bf16[16,120,128]{2,1,0:T(8,128)(2,1)} %get-tuple-element.29.refs_2_, bf16[16,120,128]{2,1,0:T(8,128)(2,1)} %get-tuple-element.32.refs_3_, ...), custom_call_target="tpu_custom_call" | custom-call | tf_op jit(solution)/shard_map/backward/pallas_call | solution.py:276
  (116 shorter events, 42.7 us)
Async XLA Ops:
  3.5 51.3 %collective-permute-start.2 = (bf16[1456,240]{0,1:T(8,128)(2,1)}, bf16[1456,240]{0,1:T(8,128)(2,1)}, u32[]{:S(2)}, u32[]{:S(2)}) collective-permute-start(bf16[1456,240]{0,1:T(8,128)(2,1)} %pad_maximum_fusion.6), channel_id=1, source_target_pairs={{0,4},{4,8},{8,12},{12,0},{1,5},{5,9},{9,13},{13,1},{2,6},{6,10},{... | collective-permute-start | bytes 2096648 | tf_op jit(solution)/shard_map/ppermute | solution.py:360
  5.0 50.2 %collective-permute-start.7 = (bf16[1456,240]{0,1:T(8,128)(2,1)}, bf16[1456,240]{0,1:T(8,128)(2,1)}, u32[]{:S(2)}, u32[]{:S(2)}) collective-permute-start(bf16[1456,240]{0,1:T(8,128)(2,1)} %pad_maximum_fusion.6), channel_id=1, source_target_pairs={{0,12},{4,0},{8,4},{12,8},{1,13},{5,1},{9,5},{13,9},{2,14},{6,2},{... | collective-permute-start | bytes 2096648 | tf_op jit(solution)/shard_map/ppermute | solution.py:360
  5.5 62.7 %collective-permute-start.12 = (bf16[1456,240]{0,1:T(8,128)(2,1)}, bf16[1456,240]{0,1:T(8,128)(2,1)}, u32[]{:S(2)}, u32[]{:S(2)}) collective-permute-start(bf16[1456,240]{0,1:T(8,128)(2,1)} %pad_maximum_fusion.6), channel_id=1, source_target_pairs={{0,8},{4,12},{8,0},{12,4},{1,9},{5,13},{9,1},{13,5},{2,10},{6,14},... | collective-permute-start | bytes 2096648 | tf_op jit(solution)/shard_map/ppermute | solution.py:360
  7.6 100.3 %collective-permute-start = (bf16[2,120,4096]{2,1,0:T(8,128)(2,1)S(1)}, bf16[2,120,4096]{2,1,0:T(8,128)(2,1)}, u32[]{:S(2)}, u32[]{:S(2)}) collective-permute-start(bf16[2,120,4096]{2,1,0:T(8,128)(2,1)S(1)} %copy-done), channel_id=1, source_target_pairs={{0,1},{1,4},{4,5},{5,8},{8,9},{9,12},{12,13},{2,3},{3,6},{6,7},{7,... | collective-permute-start | bytes 5898248 | tf_op jit(solution)/shard_map/ppermute | solution.py:23
  17.6 53.2 %copy-start.1 = (f32[4,120,64]{2,1,0:T(8,128)S(1)}, f32[4,120,64]{2,1,0:T(8,128)}, u32[]{:S(2)}) copy-start(f32[4,120,64]{2,1,0:T(8,128)} %get-tuple-element.53) | copy-start | bytes 368644
  54.7 16.6 %collective-permute-start.3 = (bf16[1456,240]{0,1:T(8,128)(2,1)}, bf16[1456,240]{0,1:T(8,128)(2,1)}, u32[]{:S(2)}, u32[]{:S(2)}) collective-permute-start(bf16[1456,240]{0,1:T(8,128)(2,1)} %collective-permute-done.2), channel_id=1, source_target_pairs={{0,1},{1,0},{2,3},{3,2},{4,5},{5,4},{6,7},{7,6},{8,9},{9,8},{10,11... | collective-permute-start | bytes 2096648 | tf_op jit(solution)/shard_map/ppermute | solution.py:364
  54.7 19.7 %collective-permute-start.4 = (bf16[1456,240]{0,1:T(8,128)(2,1)}, bf16[1456,240]{0,1:T(8,128)(2,1)}, u32[]{:S(2)}, u32[]{:S(2)}) collective-permute-start(bf16[1456,240]{0,1:T(8,128)(2,1)} %collective-permute-done.2), channel_id=1, source_target_pairs={{0,16},{16,0},{1,17},{17,1},{2,18},{18,2},{3,19},{19,3},{4,20},{20... | collective-permute-start | bytes 2096648 | tf_op jit(solution)/shard_map/ppermute | solution.py:361
  55.2 35.0 %collective-permute-start.9 = (bf16[1456,240]{0,1:T(8,128)(2,1)}, bf16[1456,240]{0,1:T(8,128)(2,1)}, u32[]{:S(2)}, u32[]{:S(2)}) collective-permute-start(bf16[1456,240]{0,1:T(8,128)(2,1)} %collective-permute-done.7), channel_id=1, source_target_pairs={{0,16},{16,0},{1,17},{17,1},{2,18},{18,2},{3,19},{19,3},{4,20},{20... | collective-permute-start | bytes 2096648 | tf_op jit(solution)/shard_map/ppermute | solution.py:361
  68.2 37.3 %collective-permute-start.14 = (bf16[1456,240]{0,1:T(8,128)(2,1)}, bf16[1456,240]{0,1:T(8,128)(2,1)}, u32[]{:S(2)}, u32[]{:S(2)}) collective-permute-start(bf16[1456,240]{0,1:T(8,128)(2,1)} %collective-permute-done.12), channel_id=1, source_target_pairs={{0,16},{16,0},{1,17},{17,1},{2,18},{18,2},{3,19},{19,3},{4,20},{20... | collective-permute-start | bytes 2096648 | tf_op jit(solution)/shard_map/ppermute | solution.py:361
  71.4 61.5 %collective-permute-start.8 = (bf16[1456,240]{0,1:T(8,128)(2,1)}, bf16[1456,240]{0,1:T(8,128)(2,1)}, u32[]{:S(2)}, u32[]{:S(2)}) collective-permute-start(bf16[1456,240]{0,1:T(8,128)(2,1)} %collective-permute-done.7), channel_id=1, source_target_pairs={{0,1},{1,0},{2,3},{3,2},{4,5},{5,4},{6,7},{7,6},{8,9},{9,8},{10,11... | collective-permute-start | bytes 2096648 | tf_op jit(solution)/shard_map/ppermute | solution.py:364
  74.4 60.0 %collective-permute-start.13 = (bf16[1456,240]{0,1:T(8,128)(2,1)}, bf16[1456,240]{0,1:T(8,128)(2,1)}, u32[]{:S(2)}, u32[]{:S(2)}) collective-permute-start(bf16[1456,240]{0,1:T(8,128)(2,1)} %collective-permute-done.12), channel_id=1, source_target_pairs={{0,1},{1,0},{2,3},{3,2},{4,5},{5,4},{6,7},{7,6},{8,9},{9,8},{10,11... | collective-permute-start | bytes 2096648 | tf_op jit(solution)/shard_map/ppermute | solution.py:364
  90.2 44.7 %collective-permute-start.5 = (bf16[1456,240]{0,1:T(8,128)(2,1)}, bf16[1456,240]{0,1:T(8,128)(2,1)}, u32[]{:S(2)}, u32[]{:S(2)}) collective-permute-start(bf16[1456,240]{0,1:T(8,128)(2,1)} %collective-permute-done.4), channel_id=1, source_target_pairs={{0,1},{1,0},{2,3},{3,2},{4,5},{5,4},{6,7},{7,6},{8,9},{9,8},{10,11... | collective-permute-start | bytes 2096648 | tf_op jit(solution)/shard_map/ppermute | solution.py:366
  105.5 30.9 %collective-permute-start.10 = (bf16[1456,240]{0,1:T(8,128)(2,1)}, bf16[1456,240]{0,1:T(8,128)(2,1)}, u32[]{:S(2)}, u32[]{:S(2)}) collective-permute-start(bf16[1456,240]{0,1:T(8,128)(2,1)} %collective-permute-done.9), channel_id=1, source_target_pairs={{0,1},{1,0},{2,3},{3,2},{4,5},{5,4},{6,7},{7,6},{8,9},{9,8},{10,11... | collective-permute-start | bytes 2096648 | tf_op jit(solution)/shard_map/ppermute | solution.py:366
  107.9 79.3 %collective-permute-start.15 = (bf16[1456,240]{0,1:T(8,128)(2,1)}, bf16[1456,240]{0,1:T(8,128)(2,1)S(1)}, u32[]{:S(2)}, u32[]{:S(2)}) collective-permute-start(bf16[1456,240]{0,1:T(8,128)(2,1)} %collective-permute-done.14), channel_id=1, source_target_pairs={{0,1},{1,0},{2,3},{3,2},{4,5},{5,4},{6,7},{7,6},{8,9},{9,8},{10,11... | collective-permute-start | bytes 2096648 | tf_op jit(solution)/shard_map/ppermute | solution.py:366
  132.8 55.6 %collective-permute-start.1 = (bf16[16,120,128]{2,1,0:T(8,128)(2,1)}, bf16[16,120,128]{2,1,0:T(8,128)(2,1)S(1)}, u32[]{:S(2)}, u32[]{:S(2)}) collective-permute-start(bf16[16,120,128]{2,1,0:T(8,128)(2,1)} %get-tuple-element.22), channel_id=1, source_target_pairs={{0,2},{2,0},{1,3},{3,1},{4,6},{6,4},{5,7},{7,5},{8,10},{10,8},{9,1... | collective-permute-start | bytes 1474568 | tf_op jit(solution)/shard_map/ppermute | solution.py:393
  134.4 70.6 %collective-permute-start.6 = (bf16[16,120,128]{2,1,0:T(8,128)(2,1)}, bf16[16,120,128]{2,1,0:T(8,128)(2,1)S(1)}, u32[]{:S(2)}, u32[]{:S(2)}) collective-permute-start(bf16[16,120,128]{2,1,0:T(8,128)(2,1)} %get-tuple-element.25), channel_id=1, source_target_pairs={{0,2},{2,0},{1,3},{3,1},{4,6},{6,4},{5,7},{7,5},{8,10},{10,8},{9,1... | collective-permute-start | bytes 1474568 | tf_op jit(solution)/shard_map/ppermute | solution.py:393
  134.9 85.6 %collective-permute-start.11 = (bf16[16,120,128]{2,1,0:T(8,128)(2,1)}, bf16[16,120,128]{2,1,0:T(8,128)(2,1)S(1)}, u32[]{:S(2)}, u32[]{:S(2)}) collective-permute-start(bf16[16,120,128]{2,1,0:T(8,128)(2,1)} %get-tuple-element.28), channel_id=1, source_target_pairs={{0,2},{2,0},{1,3},{3,1},{4,6},{6,4},{5,7},{7,5},{8,10},{10,8},{9,1... | collective-permute-start | bytes 1474568 | tf_op jit(solution)/shard_map/ppermute | solution.py:393
  136.4 100.8 %collective-permute-start.16 = (bf16[16,120,128]{2,1,0:T(8,128)(2,1)}, bf16[16,120,128]{2,1,0:T(8,128)(2,1)S(1)}, u32[]{:S(2)}, u32[]{:S(2)}) collective-permute-start(bf16[16,120,128]{2,1,0:T(8,128)(2,1)} %get-tuple-element.31), channel_id=1, source_target_pairs={{0,2},{2,0},{1,3},{3,1},{4,6},{6,4},{5,7},{7,5},{8,10},{10,8},{9,1... | collective-permute-start | bytes 1474568 | tf_op jit(solution)/shard_map/ppermute | solution.py:393
  203.4 50.4 %collective-permute-start.17 = (bf16[16,120,128]{2,1,0:T(8,128)(2,1)}, bf16[16,120,128]{2,1,0:T(8,128)(2,1)S(1)}, u32[]{:S(2)}, u32[]{:S(2)}) collective-permute-start(bf16[16,120,128]{2,1,0:T(8,128)(2,1)} %get-tuple-element.33), channel_id=1, source_target_pairs={{0,2},{2,0},{1,3},{3,1},{4,6},{6,4},{5,7},{7,5},{8,10},{10,8},{9,1... | collective-permute-start | bytes 1474568 | tf_op jit(solution)/shard_map/ppermute | solution.py:417
  219.9 33.9 %collective-permute-start.18 = (bf16[16,120,128]{2,1,0:T(8,128)(2,1)}, bf16[16,120,128]{2,1,0:T(8,128)(2,1)S(1)}, u32[]{:S(2)}, u32[]{:S(2)}) collective-permute-start(bf16[16,120,128]{2,1,0:T(8,128)(2,1)} %get-tuple-element.34), channel_id=1, source_target_pairs={{0,2},{2,0},{1,3},{3,1},{4,6},{6,4},{5,7},{7,5},{8,10},{10,8},{9,1... | collective-permute-start | bytes 1474568 | tf_op jit(solution)/shard_map/ppermute | solution.py:417
  235.7 18.1 %collective-permute-start.19 = (bf16[16,120,128]{2,1,0:T(8,128)(2,1)}, bf16[16,120,128]{2,1,0:T(8,128)(2,1)S(1)}, u32[]{:S(2)}, u32[]{:S(2)}) collective-permute-start(bf16[16,120,128]{2,1,0:T(8,128)(2,1)} %get-tuple-element.35), channel_id=1, source_target_pairs={{0,2},{2,0},{1,3},{3,1},{4,6},{6,4},{5,7},{7,5},{8,10},{10,8},{9,1... | collective-permute-start | bytes 1474568 | tf_op jit(solution)/shard_map/ppermute | solution.py:417
  252.2 11.4 %collective-permute-start.20 = (bf16[16,120,128]{2,1,0:T(8,128)(2,1)}, bf16[16,120,128]{2,1,0:T(8,128)(2,1)S(1)}, u32[]{:S(2)}, u32[]{:S(2)}) collective-permute-start(bf16[16,120,128]{2,1,0:T(8,128)(2,1)} %get-tuple-element.36), channel_id=1, source_target_pairs={{0,2},{2,0},{1,3},{3,1},{4,6},{6,4},{5,7},{7,5},{8,10},{10,8},{9,1... | collective-permute-start | bytes 1474568 | tf_op jit(solution)/shard_map/ppermute | solution.py:417
  253.8 10.7 %copy-start.5 = (bf16[16,120,128]{2,1,0:T(8,128)(2,1)}, bf16[16,120,128]{2,1,0:T(8,128)(2,1)S(1)}, u32[]{:S(2)}) copy-start(bf16[16,120,128]{2,1,0:T(8,128)(2,1)S(1)} %collective-permute-done.17.refs_4_) | copy-start | bytes 1474564
  253.8 10.7 %copy-start.7 = (bf16[16,120,128]{2,1,0:T(8,128)(2,1)}, bf16[16,120,128]{2,1,0:T(8,128)(2,1)S(1)}, u32[]{:S(2)}) copy-start(bf16[16,120,128]{2,1,0:T(8,128)(2,1)S(1)} %collective-permute-done.18.refs_5_) | copy-start | bytes 1474564
  (11 other events, 44.2 us)
